TPU v7x, 512 devices: a whole 4x4x16 slice. The times are simulated.
512 devices in a mesh: section: 2 (over y_lo), hid: 16 (over z), wid: 16 (over x, y_hi, core).
Axes of the slice: x: 4, y: 4 (y_hi: 2, y_lo: 2; y = y_hi * 2 + y_lo), z: 16, core: 2. Of those that a mesh axis runs over, the one named last changes fastest.
Arguments:
- weights: bfloat16 [2, 6144, 24576], P('section', 'hid', 'wid'), may hold values from -0.078125 to 0.078125
- preact: bfloat16 [1024, 24576], P(('section', 'hid'), 'wid'), may hold values from -6 to 6
- inputs: bfloat16 [1024, 6144], P(('section', 'wid'), 'hid'), may hold values from -6 to 6
- grad_out: bfloat16 [1024, 6144], P(('section', 'wid'), 'hid'), may hold values from -6 to 6
- row_state: float32 [2, 6144], P('section', 'hid'), may hold values from 32 to 256
- col_state: float32 [2, 24576], P('section', 'wid'), may hold values from 32 to 256
Outputs:
- input_grad: float32 [1024, 6144], P(('section', 'wid'), 'hid')
- update: float32 [2, 6144, 24576], P('section', 'hid', 'wid')
All inputs are finite; a program needn't handle non-finite values.
Results may differ from a plain program's by a relative error of at most 0.0029.
Values may be sent and summed in bfloat16 or wider, within the bound.
No kernel may reach another device: no remote copies, remote signals or barrier semaphores. Data moves between devices by JAX's collectives and lax.ppermute only.
A program may use at most 64 MiB of HBM per device.

v0:
```python
import jax
import jax.numpy as jnp
from jax import lax
from jax.sharding import PartitionSpec as P

D = 6144
FF = 24576
decay_rate = 0.9
root_half = 0.7071067811865476
inv_root_tau = 0.3989422804014327
LANES = 128


def normal_cdf(pre):
    return 0.5 * (1.0 + lax.erf(pre * root_half))


def gelu_value(pre):
    return pre * normal_cdf(pre)


def gelu_slope(pre):
    return normal_cdf(pre) + pre * jnp.exp(-0.5 * pre * pre) * inv_root_tau


def contract(left, right):
    return lax.dot_general(
        left, right, (((0,), (0,)), ((), ())), preferred_element_type=jnp.float32
    )


def exchange(blocks, axis):
    return lax.all_to_all(blocks, axis, split_axis=0, concat_axis=0, tiled=True)


def spread(block, axis):
    n = lax.axis_size(axis)
    copies = jnp.broadcast_to(block[None], (n,) + block.shape)
    return exchange(copies.reshape((n * block.shape[0],) + block.shape[1:]), axis)


def thirds(values, scalar):
    shape = (16, values.shape[0])
    row = lax.broadcasted_iota(jnp.int32, shape, 0)
    rest = jnp.where(row < 8, jnp.broadcast_to(values[None], shape), scalar)
    out = jnp.zeros(shape, jnp.float32)
    for k in range(3):
        term = lax.reduce_precision(rest, exponent_bits=8, mantissa_bits=7)
        out = jnp.where(row % 8 == k, term, out)
        rest = rest - term
    return out.astype(jnp.bfloat16)


def sum_blocks(partial, axis, groups):
    members = len(groups[0])
    columns = partial.shape[1]
    rows = partial.shape[0] // members
    power = jnp.clip(jnp.ceil(jnp.log2(jnp.maximum(jnp.max(jnp.abs(partial)), 1e-30))), -96.0, 96.0)
    coded = (partial * jnp.exp2(14.0 - power)).astype(jnp.float16).reshape(members, rows, columns)
    power = jnp.broadcast_to(power, (members, 8, columns)).astype(jnp.float16)
    taken = lax.all_to_all(
        jnp.concatenate([coded, power], axis=1),
        axis,
        split_axis=0,
        concat_axis=0,
        axis_index_groups=groups,
        tiled=True,
    )
    power = jnp.max(taken[:, rows:, :LANES].astype(jnp.float32), axis=(1, 2), keepdims=True)
    return jnp.sum(taken[:, :rows].astype(jnp.float32) * jnp.exp2(power - 14.0), axis=0)


def shards(weights, preact, inputs, grad_out, row_state, col_state):
    hid = lax.axis_size("hid")
    wid = lax.axis_size("wid")
    own_tile = weights[0]
    features, hidden = own_tile.shape
    half = hidden // 2
    rows = grad_out.shape[0]
    first = lax.axis_index("section") == 0
    even = lax.axis_index("hid") % 2 == 0
    home = lax.axis_index("section") == lax.axis_index("hid") % 2
    pair = ("section", "hid")

    def at(section, h):
        return section * hid + h

    over = [(at(h % 2, h), at(1 - h % 2, h)) for h in range(hid)]
    beside = [(at(h % 2, h ^ 1), at(h % 2, h)) for h in range(hid)]
    across = [(at(h % 2, h ^ 1), at(1 - h % 2, h)) for h in range(hid)]
    rings = [list(range(p, hid, 2)) for p in range(2)]

    def token_blocks(same, other):
        own = jnp.where(home, same, lax.ppermute(other, pair, over))
        near = lax.ppermute(same, pair, beside)
        far = lax.ppermute(other, pair, across)
        return (own, jnp.where(home, near, far))

    grad_pair = jnp.concatenate(token_blocks(grad_out, grad_out), axis=1)
    tile_near = lax.ppermute(
        own_tile[:, :half], pair, [(at(1, h), at(1, h ^ 1)) for h in range(hid)]
    )
    tile_over = lax.ppermute(own_tile[:, half:], pair, [(at(1, h), at(0, h)) for h in range(hid)])
    tile_far = lax.ppermute(
        own_tile[:, half:], pair, [(at(1, h), at(0, h ^ 1)) for h in range(hid)]
    )
    grad_half = spread(grad_pair, "wid")
    pre_own, pre_next = token_blocks(
        jnp.where(first, preact[:, half:], preact[:, :half]),
        jnp.where(first, preact[:, :half], preact[:, half:]),
    )
    grad_half, pre_own, pre_next = lax.optimization_barrier((grad_half, pre_own, pre_next))
    hidden_part = jnp.dot(
        grad_half[:, :features],
        jnp.where(first, tile_over, own_tile[:, :half]),
        preferred_element_type=jnp.float32,
    ) + jnp.dot(
        grad_half[:, features:],
        jnp.where(first, tile_far, tile_near),
        preferred_element_type=jnp.float32,
    )
    hidden_share = sum_blocks(hidden_part, "hid", rings)
    pre_half = jnp.concatenate(
        [jnp.where(even, pre_own, pre_next), jnp.where(even, pre_next, pre_own)]
    )
    pre_taken = lax.ppermute(pre_half, "section", [(0, 1)])
    act_share = gelu_value(
        jnp.concatenate([pre_half, pre_taken], axis=1).astype(jnp.float32)
    ).astype(jnp.bfloat16)
    pre_share = (hidden_share * gelu_slope(pre_half.astype(jnp.float32))).astype(jnp.bfloat16)
    pre_share = jnp.concatenate([lax.ppermute(pre_share, "section", [(1, 0)]), pre_share], axis=1)
    right = lax.all_gather(jnp.where(first, pre_share, act_share), "hid", axis=0, tiled=True)
    kept = jnp.where(first, inputs, grad_out)
    given = jnp.where(first, grad_out, inputs)
    taken = lax.ppermute(given, "section", [(0, 1), (1, 0)])
    left_own = jnp.concatenate([jnp.where(first, kept, taken), jnp.where(first, taken, kept)])
    left = jnp.swapaxes(
        spread(left_own, "wid").reshape(wid // 2, 2, 2, rows, features), 1, 2
    ).reshape(2 * wid * rows, features)
    gradient = contract(left, right)
    squares = gradient * gradient
    row_local = jnp.sum(squares, axis=1)
    col_local = jnp.sum(squares, axis=0)
    row_prev = row_state[0]
    col_prev = col_state[0]
    scalars = jnp.stack([jnp.sum(row_local), jnp.sum(row_prev)])
    tail = jnp.concatenate([scalars, jnp.zeros((4 * LANES - 2,), jnp.float32)])
    packed = jnp.concatenate([col_local, tail]).reshape(-1, LANES)
    over_hid = jnp.sum(spread(packed, "hid").reshape((hid,) + packed.shape), axis=0).reshape(-1)
    col_total = over_hid[:hidden]
    square_sum, prev_sum = (over_hid[hidden], over_hid[hidden + 1])
    partial = lax.dot_general(
        right, own_tile, (((1,), (1,)), ((), ())), preferred_element_type=jnp.float32
    ).astype(jnp.bfloat16)
    blocks = jnp.swapaxes(partial.reshape(wid // 2, 2, 2, rows, features), 1, 2)
    extra = thirds(row_local, square_sum)
    blocks = jnp.concatenate(
        [
            blocks.reshape(wid, 2 * rows, features),
            jnp.broadcast_to(extra[None], (wid,) + extra.shape),
        ],
        axis=1,
    )
    over_wid = jnp.sum(exchange(blocks, "wid").astype(jnp.float32), axis=0)
    input_sum = jnp.where(
        first, over_wid[:rows], lax.ppermute(over_wid[rows : 2 * rows], "section", [(0, 1)])
    )
    input_grad = input_sum + grad_out.astype(jnp.float32)
    row_total = jnp.sum(over_wid[2 * rows : 2 * rows + 8], axis=0)
    square_total = jnp.sum(over_wid[2 * rows + 8 :, 0])
    row_moment = decay_rate * row_prev + (1.0 - decay_rate) / FF * row_total
    col_moment = decay_rate * col_prev + (1.0 - decay_rate) / D * col_total
    row_mean = decay_rate / D * prev_sum + (1.0 - decay_rate) / FF / D * square_total
    update = gradient * lax.rsqrt(row_moment[:, None] * col_moment[None, :] / row_mean)
    return (input_grad, update[None])


def solution(mesh):
    placed = (
        P("section", "hid", "wid"),
        P(("section", "hid"), "wid"),
        P(("section", "wid"), "hid"),
        P(("section", "wid"), "hid"),
        P("section", "hid"),
        P("section", "wid"),
    )
    return jax.shard_map(
        shards,
        mesh=mesh,
        in_specs=placed,
        out_specs=(P(("section", "wid"), "hid"), P("section", "hid", "wid")),
        check_vma=False,
    )
```

profile of v0, /device:TPU:8, one launch (start us, length us, event | category | flops | bytes accessed | tf_op | source)
XLA Modules:
  0.0 273.0 jit_solution(15380726887972053118)
XLA Ops:
  8.6 4.9 %collective-permute-start.1 = (bf16[32,384]{1,0:T(8,128)(2,1)}, bf16[32,384]{1,0:T(8,128)(2,1)S(1)}, u32[]{:S(2)}, u32[]{:S(2)}) collective-permute-start(bf16[32,384]{1,0:T(8,128)(2,1)} %param.9), channel_id=1, source_target_pairs={{16,0},{256,272},{48,32},{288,304},{80,64},{320,336},{112,96},{352... | collective-permute-start | bytes 73736 | tf_op jit(solution)/shard_map/ppermute | solution.py:95
  13.5 6.2 %collective-permute-start.2 = (bf16[32,384]{1,0:T(8,128)(2,1)}, bf16[32,384]{1,0:T(8,128)(2,1)S(1)}, u32[]{:S(2)}, u32[]{:S(2)}) collective-permute-start(bf16[32,384]{1,0:T(8,128)(2,1)} %param.9), channel_id=1, source_target_pairs={{16,256},{256,16},{48,288},{288,48},{80,320},{320,80},{112,352},{3... | collective-permute-start | bytes 73736 | tf_op jit(solution)/shard_map/ppermute | solution.py:96
  23.7 2.9 %collective-permute-start.7 = (bf16[384,768]{1,0:T(8,128)(2,1)S(1)}, bf16[384,768]{1,0:T(8,128)(2,1)}, u32[]{:S(2)}, u32[]{:S(2)}) collective-permute-start(bf16[384,768]{1,0:T(8,128)(2,1)S(1)} %get-tuple-element.16), channel_id=1, source_target_pairs={{256,16},{272,0},{288,48},{304,32},{320,80},{336,64},{352,112},{36... | collective-permute-start | bytes 1769480 | tf_op jit(solution)/shard_map/ppermute | solution.py:104
  26.6 5.3 %collective-permute-start.8 = (bf16[384,768]{1,0:T(8,128)(2,1)S(1)}, bf16[384,768]{1,0:T(8,128)(2,1)}, u32[]{:S(2)}, u32[]{:S(2)}) collective-permute-start(bf16[384,768]{1,0:T(8,128)(2,1)S(1)} %get-tuple-element.15), channel_id=1, source_target_pairs={{256,272},{272,256},{288,304},{304,288},{320,336},{336,320},{352,3... | collective-permute-start | bytes 1769480 | tf_op jit(solution)/shard_map/ppermute | solution.py:100
  33.6 3.6 %all-to-all-start = ((bf16[16,32,768]{2,1,0:T(8,128)(2,1)}), bf16[16,32,768]{2,1,0:T(8,128)(2,1)S(1)}, u32[]{:S(2)}, u32[]{:S(2)}) async-start(bf16[16,32,768]{2,1,0:T(8,128)(2,1)} %broadcast_in_dim.22), calls=%async_computation | async-start | bytes 1572864 | tf_op jit(solution)/shard_map/all_to_all | solution.py:33
  38.7 1.9 collective-permute-start.5
  40.7 4.1 %collective-permute-start.6 = (bf16[384,768]{1,0:T(8,128)(2,1)S(1)}, bf16[384,768]{1,0:T(8,128)(2,1)}, u32[]{:S(2)}, u32[]{:S(2)}) collective-permute-start(bf16[384,768]{1,0:T(8,128)(2,1)S(1)} %get-tuple-element.16), channel_id=1, source_target_pairs={{256,0},{272,16},{288,32},{304,48},{320,64},{336,80},{352,96},{368... | collective-permute-start | bytes 1769480 | tf_op jit(solution)/shard_map/ppermute | solution.py:103
  44.8 2.9 %collective-permute-done.3 = bf16[32,768]{1,0:T(8,128)(2,1)S(1)} collective-permute-done((bf16[32,768]{1,0:T(8,128)(2,1)S(1)}, bf16[32,768]{1,0:T(8,128)(2,1)S(1)}, u32[]{:S(2)}, u32[]{:S(2)}) %collective-permute-start.3) | collective-permute-done | bytes 49184 | tf_op jit(solution)/shard_map/ppermute | solution.py:94
  48.3 3.9 %collective-permute-start.4 = (bf16[32,768]{1,0:T(8,128)(2,1)S(1)}, bf16[32,768]{1,0:T(8,128)(2,1)S(1)}, u32[]{:S(2)}, u32[]{:S(2)}) collective-permute-start(bf16[32,768]{1,0:T(8,128)(2,1)S(1)} %get-tuple-element.14), channel_id=1, source_target_pairs={{16,0},{256,272},{48,32},{288,304},{80,64},{320,336},{112,96},{352... | collective-permute-start | bytes 147464 | tf_op jit(solution)/shard_map/ppermute | solution.py:95
  56.2 5.1 %collective-permute-done.6 = bf16[384,768]{1,0:T(8,128)(2,1)} collective-permute-done((bf16[384,768]{1,0:T(8,128)(2,1)S(1)}, bf16[384,768]{1,0:T(8,128)(2,1)}, u32[]{:S(2)}, u32[]{:S(2)}) %collective-permute-start.6) | collective-permute-done | bytes 589856 | tf_op jit(solution)/shard_map/ppermute | solution.py:103
  64.5 14.1 %all-to-all-start.1 = ((f16[8,72,768]{2,1,0:T(8,128)(2,1)}), f16[8,72,768]{2,1,0:T(8,128)(2,1)S(1)}, u32[]{:S(2)}, u32[]{:S(2)}) async-start(f16[8,72,768]{2,1,0:T(8,128)(2,1)} %concatenate.25), calls=%async_computation.1 | async-start | bytes 1769472 | tf_op jit(solution)/shard_map/all_to_all | solution.py:61
  80.0 29.8 %all-to-all-done.1 = f16[8,72,768]{2,1,0:T(8,128)(2,1)S(1)} async-done(((f16[8,72,768]{2,1,0:T(8,128)(2,1)}), f16[8,72,768]{2,1,0:T(8,128)(2,1)S(1)}, u32[]{:S(2)}, u32[]{:S(2)}) %all-to-all-start.1) | async-done | bytes 884768 | tf_op jit(solution)/shard_map/all_to_all | solution.py:61
  110.4 5.6 %collective-permute-start.9 = (bf16[64,768]{1,0:T(8,128)(2,1)S(1)}, bf16[64,768]{1,0:T(8,128)(2,1)S(1)}, u32[]{:S(2)}, u32[]{:S(2)}) collective-permute-start(bf16[64,768]{1,0:T(8,128)(2,1)S(1)} %fusion.19), channel_id=1, source_target_pairs={{256,0},{257,1},{258,2},{259,3},{260,4},{261,5},{262,6},{263,7},{2... | collective-permute-start | bytes 294920 | tf_op jit(solution)/shard_map/ppermute | solution.py:131
  115.9 2.2 collective-permute-done.9
  119.9 5.8 %all-to-all-start.2 = ((bf16[16,64,384]{2,1,0:T(8,128)(2,1)}), bf16[16,64,384]{2,1,0:T(8,128)(2,1)S(1)}, u32[]{:S(2)}, u32[]{:S(2)}) async-start(bf16[16,64,384]{2,1,0:T(8,128)(2,1)} %broadcast_in_dim.23), calls=%async_computation.2 | async-start | bytes 1572864 | tf_op jit(solution)/shard_map/all_to_all | solution.py:33
  126.5 14.4 %all-to-all-done.2 = bf16[16,64,384]{2,1,0:T(8,128)(2,1)S(1)} async-done(((bf16[16,64,384]{2,1,0:T(8,128)(2,1)}), bf16[16,64,384]{2,1,0:T(8,128)(2,1)S(1)}, u32[]{:S(2)}, u32[]{:S(2)}) %all-to-all-start.2) | async-done | bytes 786464 | tf_op jit(solution)/shard_map/all_to_all | solution.py:33
  141.0 63.7 %all-gather.2.cloned.1.call-done = bf16[1024,1536]{1,0:T(8,128)(2,1)} async-done(((bf16[64,1536]{1,0:T(8,128)(2,1)}), bf16[1024,1536]{1,0:T(8,128)(2,1)}) %all-gather.2.cloned.1.call-update) | async-done | bytes 3145744 | tf_op jit(solution)/shard_map/all_gather | solution.py:132
  204.8 5.4 %multiply_reduce_fusion.2 = (f32[384]{0:T(512)S(1)}, f32[1536]{0:T(1024)S(1)}, f32[]{:T(128)}, f32[384,1536]{1,0:T(8,128)}) fusion(bf16[1024,384]{1,0:T(8,128)(2,1)S(1)} %bitcast.38, bf16[1024,1536]{1,0:T(8,128)(2,1)} %all-gather.2.cloned.1.call-done), kind=kOutput, calls=%fused_computation.3 | convolution fusion | flops 1210316928 | bytes 6299140 | tf_op jit(solution)/shard_map/dot_general | solution.py:27
  212.2 7.8 %all-to-all-start.3 = ((f32[16,16,128]{2,1,0:T(8,128)}), f32[16,16,128]{2,1,0:T(8,128)S(1)}, u32[]{:S(2)}, u32[]{:S(2)}) async-start(f32[16,16,128]{2,1,0:T(8,128)} %broadcast_in_dim.27), calls=%async_computation.3 | async-start | bytes 262144 | tf_op jit(solution)/shard_map/all_to_all | solution.py:33
  219.9 3.7 %convolution_convert_fusion = bf16[1024,384]{1,0:T(8,128)(2,1)S(1)} fusion(bf16[1024,1536]{1,0:T(8,128)(2,1)} %all-gather.2.cloned.1.call-done, bf16[1,384,1536]{2,1,0:T(8,128)(2,1)S(1)} %copy-done), kind=kOutput, calls=%fused_computation.9 | convolution fusion | flops 1208352768 | bytes 5111808 | tf_op jit(solution)/shard_map/dot_general | solution.py:152
  223.8 9.3 %all-to-all-done.3 = f32[16,16,128]{2,1,0:T(8,128)S(1)} async-done(((f32[16,16,128]{2,1,0:T(8,128)}), f32[16,16,128]{2,1,0:T(8,128)S(1)}, u32[]{:S(2)}, u32[]{:S(2)}) %all-to-all-start.3) | async-done | bytes 131104 | tf_op jit(solution)/shard_map/all_to_all | solution.py:33
  235.4 6.0 %all-to-all-start.4 = ((bf16[16,80,384]{2,1,0:T(8,128)(2,1)}), bf16[16,80,384]{2,1,0:T(8,128)(2,1)S(1)}, u32[]{:S(2)}, u32[]{:S(2)}) async-start(bf16[16,80,384]{2,1,0:T(8,128)(2,1)} %pad_maximum_fusion), calls=%async_computation.4 | async-start | bytes 1966080 | tf_op jit(solution)/shard_map/all_to_all | solution.py:33
  242.2 16.5 %all-to-all-done.4 = bf16[16,80,384]{2,1,0:T(8,128)(2,1)S(1)} async-done(((bf16[16,80,384]{2,1,0:T(8,128)(2,1)}), bf16[16,80,384]{2,1,0:T(8,128)(2,1)S(1)}, u32[]{:S(2)}, u32[]{:S(2)}) %all-to-all-start.4) | async-done | bytes 983072 | tf_op jit(solution)/shard_map/all_to_all | solution.py:33
  263.3 2.2 collective-permute-done.12
  (85 shorter events, 29.0 us)
Async XLA Ops:
  7.2 24.8 %copy-start.3 = (bf16[32,384]{1,0:T(8,128)(2,1)S(1)}, bf16[32,384]{1,0:T(8,128)(2,1)}, u32[]{:S(2)}) copy-start(bf16[32,384]{1,0:T(8,128)(2,1)} %param.9) | copy-start | bytes 73732
  7.2 24.8 %copy-start.7 = (bf16[32,384]{1,0:T(8,128)(2,1)S(1)}, bf16[32,384]{1,0:T(8,128)(2,1)}, u32[]{:S(2)}) copy-start(bf16[32,384]{1,0:T(8,128)(2,1)} %param.8) | copy-start | bytes 73732
  7.2 24.8 %collective-permute-start = (bf16[32,384]{1,0:T(8,128)(2,1)}, bf16[32,384]{1,0:T(8,128)(2,1)S(1)}, u32[]{:S(2)}, u32[]{:S(2)}) collective-permute-start(bf16[32,384]{1,0:T(8,128)(2,1)} %param.9), channel_id=1, source_target_pairs={{0,256},{272,16},{32,288},{304,48},{64,320},{336,80},{96,352},{368... | collective-permute-start | bytes 73736 | tf_op jit(solution)/shard_map/ppermute | solution.py:94
  8.6 24.0 %collective-permute-start.1 = (bf16[32,384]{1,0:T(8,128)(2,1)}, bf16[32,384]{1,0:T(8,128)(2,1)S(1)}, u32[]{:S(2)}, u32[]{:S(2)}) collective-permute-start(bf16[32,384]{1,0:T(8,128)(2,1)} %param.9), channel_id=1, source_target_pairs={{16,0},{256,272},{48,32},{288,304},{80,64},{320,336},{112,96},{352... | collective-permute-start | bytes 73736 | tf_op jit(solution)/shard_map/ppermute | solution.py:95
  13.5 19.1 %collective-permute-start.2 = (bf16[32,384]{1,0:T(8,128)(2,1)}, bf16[32,384]{1,0:T(8,128)(2,1)S(1)}, u32[]{:S(2)}, u32[]{:S(2)}) collective-permute-start(bf16[32,384]{1,0:T(8,128)(2,1)} %param.9), channel_id=1, source_target_pairs={{16,256},{256,16},{48,288},{288,48},{80,320},{320,80},{112,352},{3... | collective-permute-start | bytes 73736 | tf_op jit(solution)/shard_map/ppermute | solution.py:96
  20.5 6.2 %collective-permute-start.11 = (bf16[32,384]{1,0:T(8,128)(2,1)S(1)}, bf16[32,384]{1,0:T(8,128)(2,1)S(1)}, u32[]{:S(2)}, u32[]{:S(2)}) collective-permute-start(bf16[32,384]{1,0:T(8,128)(2,1)S(1)} %broadcast_select_fusion.10), channel_id=1, source_target_pairs={{0,256},{256,0},{1,257},{257,1},{2,258},{258,2},{3,259},{259,3},{4... | collective-permute-start | bytes 73736 | tf_op jit(solution)/shard_map/ppermute | solution.py:135
  23.7 30.8 %collective-permute-start.7 = (bf16[384,768]{1,0:T(8,128)(2,1)S(1)}, bf16[384,768]{1,0:T(8,128)(2,1)}, u32[]{:S(2)}, u32[]{:S(2)}) collective-permute-start(bf16[384,768]{1,0:T(8,128)(2,1)S(1)} %get-tuple-element.16), channel_id=1, source_target_pairs={{256,16},{272,0},{288,48},{304,32},{320,80},{336,64},{352,112},{36... | collective-permute-start | bytes 1769480 | tf_op jit(solution)/shard_map/ppermute | solution.py:104
  26.6 27.9 %collective-permute-start.8 = (bf16[384,768]{1,0:T(8,128)(2,1)S(1)}, bf16[384,768]{1,0:T(8,128)(2,1)}, u32[]{:S(2)}, u32[]{:S(2)}) collective-permute-start(bf16[384,768]{1,0:T(8,128)(2,1)S(1)} %get-tuple-element.15), channel_id=1, source_target_pairs={{256,272},{272,256},{288,304},{304,288},{320,336},{336,320},{352,3... | collective-permute-start | bytes 1769480 | tf_op jit(solution)/shard_map/ppermute | solution.py:100
  33.6 20.9 %all-to-all-start = ((bf16[16,32,768]{2,1,0:T(8,128)(2,1)}), bf16[16,32,768]{2,1,0:T(8,128)(2,1)S(1)}, u32[]{:S(2)}, u32[]{:S(2)}) async-start(bf16[16,32,768]{2,1,0:T(8,128)(2,1)} %broadcast_in_dim.22), calls=%async_computation | async-start | bytes 1572864 | tf_op jit(solution)/shard_map/all_to_all | solution.py:33
  37.3 10.4 %collective-permute-start.3 = (bf16[32,768]{1,0:T(8,128)(2,1)S(1)}, bf16[32,768]{1,0:T(8,128)(2,1)S(1)}, u32[]{:S(2)}, u32[]{:S(2)}) collective-permute-start(bf16[32,768]{1,0:T(8,128)(2,1)S(1)} %broadcast_select_fusion.2), channel_id=1, source_target_pairs={{0,256},{272,16},{32,288},{304,48},{64,320},{336,80},{96,352},{368... | collective-permute-start | bytes 147464 | tf_op jit(solution)/shard_map/ppermute | solution.py:94
  38.7 13.5 %collective-permute-start.5 = (bf16[32,768]{1,0:T(8,128)(2,1)S(1)}, bf16[32,768]{1,0:T(8,128)(2,1)S(1)}, u32[]{:S(2)}, u32[]{:S(2)}) collective-permute-start(bf16[32,768]{1,0:T(8,128)(2,1)S(1)} %broadcast_select_fusion.2), channel_id=1, source_target_pairs={{16,256},{256,16},{48,288},{288,48},{80,320},{320,80},{112,352},{3... | collective-permute-start | bytes 147464 | tf_op jit(solution)/shard_map/ppermute | solution.py:96
  40.7 20.7 %collective-permute-start.6 = (bf16[384,768]{1,0:T(8,128)(2,1)S(1)}, bf16[384,768]{1,0:T(8,128)(2,1)}, u32[]{:S(2)}, u32[]{:S(2)}) collective-permute-start(bf16[384,768]{1,0:T(8,128)(2,1)S(1)} %get-tuple-element.16), channel_id=1, source_target_pairs={{256,0},{272,16},{288,32},{304,48},{320,64},{336,80},{352,96},{368... | collective-permute-start | bytes 1769480 | tf_op jit(solution)/shard_map/ppermute | solution.py:103
  48.3 5.6 %collective-permute-start.4 = (bf16[32,768]{1,0:T(8,128)(2,1)S(1)}, bf16[32,768]{1,0:T(8,128)(2,1)S(1)}, u32[]{:S(2)}, u32[]{:S(2)}) collective-permute-start(bf16[32,768]{1,0:T(8,128)(2,1)S(1)} %get-tuple-element.14), channel_id=1, source_target_pairs={{16,0},{256,272},{48,32},{288,304},{80,64},{320,336},{112,96},{352... | collective-permute-start | bytes 147464 | tf_op jit(solution)/shard_map/ppermute | solution.py:95
  64.5 54.4 %copy-start.8 = (bf16[32,384]{1,0:T(8,128)(2,1)S(1)}, bf16[32,384]{1,0:T(8,128)(2,1)}, u32[]{:S(2)}) copy-start(bf16[32,384]{1,0:T(8,128)(2,1)} %get-tuple-element.19) | copy-start | bytes 73732
  64.5 54.4 %copy-start.9 = (bf16[32,384]{1,0:T(8,128)(2,1)S(1)}, bf16[32,384]{1,0:T(8,128)(2,1)}, u32[]{:S(2)}) copy-start(bf16[32,384]{1,0:T(8,128)(2,1)} %get-tuple-element.20) | copy-start | bytes 73732
  64.5 45.3 %all-to-all-start.1 = ((f16[8,72,768]{2,1,0:T(8,128)(2,1)}), f16[8,72,768]{2,1,0:T(8,128)(2,1)S(1)}, u32[]{:S(2)}, u32[]{:S(2)}) async-start(f16[8,72,768]{2,1,0:T(8,128)(2,1)} %concatenate.25), calls=%async_computation.1 | async-start | bytes 1769472 | tf_op jit(solution)/shard_map/all_to_all | solution.py:61
  78.6 126.2 %all-gather.2.cloned.1.call-start = ((), (), s32[]{:S(2)}) async-start(), calls=%async_computation.5 | async-start | bytes 3342336 | tf_op jit(solution)/shard_map/all_gather | solution.py:132
  78.7 37.2 %collective-permute-start.10 = (bf16[64,768]{1,0:T(8,128)(2,1)S(1)}, bf16[64,768]{1,0:T(8,128)(2,1)S(1)}, u32[]{:S(2)}, u32[]{:S(2)}) collective-permute-start(bf16[64,768]{1,0:T(8,128)(2,1)S(1)} %pad_maximum_fusion.1), channel_id=1, source_target_pairs={{0,256},{1,257},{2,258},{3,259},{4,260},{5,261},{6,262},{7,263},{8... | collective-permute-start | bytes 294920 | tf_op jit(solution)/shard_map/ppermute | solution.py:126
  110.4 7.8 %collective-permute-start.9 = (bf16[64,768]{1,0:T(8,128)(2,1)S(1)}, bf16[64,768]{1,0:T(8,128)(2,1)S(1)}, u32[]{:S(2)}, u32[]{:S(2)}) collective-permute-start(bf16[64,768]{1,0:T(8,128)(2,1)S(1)} %fusion.19), channel_id=1, source_target_pairs={{256,0},{257,1},{258,2},{259,3},{260,4},{261,5},{262,6},{263,7},{2... | collective-permute-start | bytes 294920 | tf_op jit(solution)/shard_map/ppermute | solution.py:131
  119.9 21.0 %all-to-all-start.2 = ((bf16[16,64,384]{2,1,0:T(8,128)(2,1)}), bf16[16,64,384]{2,1,0:T(8,128)(2,1)S(1)}, u32[]{:S(2)}, u32[]{:S(2)}) async-start(bf16[16,64,384]{2,1,0:T(8,128)(2,1)} %broadcast_in_dim.23), calls=%async_computation.2 | async-start | bytes 1572864 | tf_op jit(solution)/shard_map/all_to_all | solution.py:33
  212.2 20.9 %all-to-all-start.3 = ((f32[16,16,128]{2,1,0:T(8,128)}), f32[16,16,128]{2,1,0:T(8,128)S(1)}, u32[]{:S(2)}, u32[]{:S(2)}) async-start(f32[16,16,128]{2,1,0:T(8,128)} %broadcast_in_dim.27), calls=%async_computation.3 | async-start | bytes 262144 | tf_op jit(solution)/shard_map/all_to_all | solution.py:33
  235.4 26.1 %copy-start.1 = (f32[384,1536]{1,0:T(8,128)S(1)}, f32[384,1536]{1,0:T(8,128)}, u32[]{:S(2)}) copy-start(f32[384,1536]{1,0:T(8,128)} %get-tuple-element.26) | copy-start | bytes 7077892
  235.4 23.3 %all-to-all-start.4 = ((bf16[16,80,384]{2,1,0:T(8,128)(2,1)}), bf16[16,80,384]{2,1,0:T(8,128)(2,1)S(1)}, u32[]{:S(2)}, u32[]{:S(2)}) async-start(bf16[16,80,384]{2,1,0:T(8,128)(2,1)} %pad_maximum_fusion), calls=%async_computation.4 | async-start | bytes 1966080 | tf_op jit(solution)/shard_map/all_to_all | solution.py:33
  259.6 6.0 %collective-permute-start.12 = (f32[32,384]{1,0:T(8,128)S(1)}, f32[32,384]{1,0:T(8,128)S(1)}, u32[]{:S(2)}, u32[]{:S(2)}) collective-permute-start(f32[32,384]{1,0:T(8,128)S(1)} %slice.71), channel_id=1, source_target_pairs={{0,256},{1,257},{2,258},{3,259},{4,260},{5,261},{6,262},{7,263},{8... | collective-permute-start | bytes 147464 | tf_op jit(solution)/shard_map/ppermute | solution.py:166
  (7 other events, 95.4 us)
Sparse Core Ops, SparseCore 0:
  119.0 85.6 all-gather.1
where the time goes:
time: 274 us; the launch traced here: 273 us
  waiting for transfers between devices  148 us (54%)
  starting transfers between devices  79.5 us (29%)
  between operations  16.5 us (6%)
  matrix products  11.9 us (4%)
  other arithmetic  9.82 us (4%)
  local copies, waits for them, and re-layouts  7.24 us (3%)
    all_gather x1, waiting for transfers between devices, shards(): lax.all_gather(jnp.where(first, pre_share, act_share), 'hid', axis=0, til...  63.7 us
    all_to_all x4, waiting for transfers between devices, exchange(): return lax.all_to_all(blocks, axis, split_axis=0, concat_axis=0, tiled=True)  40.3 us
    all_to_all x1, waiting for transfers between devices, sum_blocks(): lax.all_to_all(jnp.concatenate([coded, power], axis=1), axis, split_axis=...  29.8 us
    all_to_all x4, starting transfers between devices, exchange(): return lax.all_to_all(blocks, axis, split_axis=0, concat_axis=0, tiled=True)  23.3 us
    all_to_all x1, starting transfers between devices, sum_blocks(): lax.all_to_all(jnp.concatenate([coded, power], axis=1), axis, split_axis=...  14.1 us
    ppermute x2, starting transfers between devices, token_blocks(): near = lax.ppermute(same, pair, beside)  8.77 us
    ppermute x2, starting transfers between devices, token_blocks(): far = lax.ppermute(other, pair, across)  8.11 us
    ppermute x1, starting transfers between devices, shards(): lax.ppermute(pre_share, 'section', [(1, 0)])  5.56 us
  transfers between devices with their start and end apart: 19, of which 10 were waited for; matrix products, arithmetic and copies ran while one was open for 5% of the time, Pallas kernels for 0%

commit v1 on v0

--- a/solution.py
+++ b/solution.py
@@ -129,7 +129,12 @@
     ).astype(jnp.bfloat16)
     pre_share = (hidden_share * gelu_slope(pre_half.astype(jnp.float32))).astype(jnp.bfloat16)
     pre_share = jnp.concatenate([lax.ppermute(pre_share, "section", [(1, 0)]), pre_share], axis=1)
-    right = lax.all_gather(jnp.where(first, pre_share, act_share), "hid", axis=0, tiled=True)
+    right = jnp.concatenate(
+        lax.all_to_all(
+            jnp.stack([jnp.where(first, pre_share, act_share)] * lax.axis_size("hid")), "hid", 0, 0
+        ),
+        axis=0,
+    )
     kept = jnp.where(first, inputs, grad_out)
     given = jnp.where(first, grad_out, inputs)
     taken = lax.ppermute(given, "section", [(0, 1), (1, 0)])

time: 274 us -> 349 us (1.27)
  the two profiles are of different devices: /device:TPU:8 before, /device:TPU:1 now
where the time goes in v1:
time: 349 us; the launch traced here: 348 us
  waiting for transfers between devices  216 us (62%)
  starting transfers between devices  97.7 us (28%)
  matrix products  11.6 us (3%)
  local copies, waits for them, and re-layouts  11.1 us (3%)
  other arithmetic  9.05 us (3%)
    all_to_all x1, waiting for transfers between devices, shards(): lax.all_to_all(jnp.stack([jnp.where(first, pre_share, act_share)] * lax.a...  134 us
    all_to_all x4, starting transfers between devices, exchange(): return lax.all_to_all(blocks, axis, split_axis=0, concat_axis=0, tiled=True)  35.1 us
    all_to_all x1, waiting for transfers between devices, sum_blocks(): lax.all_to_all(jnp.concatenate([coded, power], axis=1), axis, split_axis=...  29.3 us
    all_to_all x4, waiting for transfers between devices, exchange(): return lax.all_to_all(blocks, axis, split_axis=0, concat_axis=0, tiled=True)  26.9 us
    all_to_all x1, starting transfers between devices, shards(): lax.all_to_all(jnp.stack([jnp.where(first, pre_share, act_share)] * lax.a...  19.5 us
    all_to_all x1, starting transfers between devices, sum_blocks(): lax.all_to_all(jnp.concatenate([coded, power], axis=1), axis, split_axis=...  13.6 us
    ppermute x2, starting transfers between devices, token_blocks(): own = jnp.where(home, same, lax.ppermute(other, pair, over))  11.1 us
    ppermute x1, waiting for transfers between devices, shards(): lax.ppermute(pre_share, 'section', [(1, 0)])  9.03 us
  transfers between devices with their start and end apart: 19, of which 9 were waited for; matrix products, arithmetic and copies ran while one was open for 5% of the time, Pallas kernels for 0%

profile of v1, /device:TPU:1, one launch (start us, length us, event | category | flops | bytes accessed | tf_op | source)
XLA Modules:
  0.0 348.2 jit_solution(4691728486092756838)
XLA Ops:
  0.7 4.2 %collective-permute-start = (bf16[32,384]{1,0:T(8,128)(2,1)}, bf16[32,384]{1,0:T(8,128)(2,1)S(1)}, u32[]{:S(2)}, u32[]{:S(2)}) collective-permute-start(bf16[32,384]{1,0:T(8,128)(2,1)} %param.9), channel_id=1, source_target_pairs={{0,256},{272,16},{32,288},{304,48},{64,320},{336,80},{96,352},{368... | collective-permute-start | bytes 73736 | tf_op jit(solution)/shard_map/ppermute | solution.py:94
  7.5 6.4 %collective-permute-start.11 = (bf16[32,384]{1,0:T(8,128)(2,1)S(1)}, bf16[32,384]{1,0:T(8,128)(2,1)S(1)}, u32[]{:S(2)}, u32[]{:S(2)}) collective-permute-start(bf16[32,384]{1,0:T(8,128)(2,1)S(1)} %broadcast_select_fusion.10), channel_id=1, source_target_pairs={{0,256},{256,0},{1,257},{257,1},{2,258},{258,2},{3,259},{259,3},{4... | collective-permute-start | bytes 73736 | tf_op jit(solution)/shard_map/ppermute | solution.py:140
  19.9 8.4 %all-to-all-start = ((bf16[16,32,768]{2,1,0:T(8,128)(2,1)}), bf16[16,32,768]{2,1,0:T(8,128)(2,1)S(1)}, u32[]{:S(2)}, u32[]{:S(2)}) async-start(bf16[16,32,768]{2,1,0:T(8,128)(2,1)} %broadcast_in_dim.22), calls=%async_computation | async-start | bytes 1572864 | tf_op jit(solution)/shard_map/all_to_all | solution.py:33
  28.4 7.0 %collective-permute-start.3 = (bf16[32,768]{1,0:T(8,128)(2,1)S(1)}, bf16[32,768]{1,0:T(8,128)(2,1)S(1)}, u32[]{:S(2)}, u32[]{:S(2)}) collective-permute-start(bf16[32,768]{1,0:T(8,128)(2,1)S(1)} %broadcast_select_fusion.2), channel_id=1, source_target_pairs={{0,256},{272,16},{32,288},{304,48},{64,320},{336,80},{96,352},{368... | collective-permute-start | bytes 147464 | tf_op jit(solution)/shard_map/ppermute | solution.py:94
  37.4 3.7 %collective-permute-done.3 = bf16[32,768]{1,0:T(8,128)(2,1)S(1)} collective-permute-done((bf16[32,768]{1,0:T(8,128)(2,1)S(1)}, bf16[32,768]{1,0:T(8,128)(2,1)S(1)}, u32[]{:S(2)}, u32[]{:S(2)}) %collective-permute-start.3) | collective-permute-done | bytes 49184 | tf_op jit(solution)/shard_map/ppermute | solution.py:94
  43.0 6.7 %collective-permute-done.4 = bf16[32,768]{1,0:T(8,128)(2,1)S(1)} collective-permute-done((bf16[32,768]{1,0:T(8,128)(2,1)S(1)}, bf16[32,768]{1,0:T(8,128)(2,1)S(1)}, u32[]{:S(2)}, u32[]{:S(2)}) %collective-permute-start.4) | collective-permute-done | bytes 49184 | tf_op jit(solution)/shard_map/ppermute | solution.py:95
  51.9 5.9 %collective-permute-done.6 = bf16[384,768]{1,0:T(8,128)(2,1)} collective-permute-done((bf16[384,768]{1,0:T(8,128)(2,1)S(1)}, bf16[384,768]{1,0:T(8,128)(2,1)}, u32[]{:S(2)}, u32[]{:S(2)}) %collective-permute-start.6) | collective-permute-done | bytes 589856 | tf_op jit(solution)/shard_map/ppermute | solution.py:103
  57.9 2.3 abs_reduce_fusion
  62.1 13.6 %all-to-all-start.1 = ((f16[8,72,768]{2,1,0:T(8,128)(2,1)}), f16[8,72,768]{2,1,0:T(8,128)(2,1)S(1)}, u32[]{:S(2)}, u32[]{:S(2)}) async-start(f16[8,72,768]{2,1,0:T(8,128)(2,1)} %concatenate.29), calls=%async_computation.1 | async-start | bytes 1769472 | tf_op jit(solution)/shard_map/all_to_all | solution.py:61
  77.1 29.3 %all-to-all-done.1 = f16[8,72,768]{2,1,0:T(8,128)(2,1)S(1)} async-done(((f16[8,72,768]{2,1,0:T(8,128)(2,1)}), f16[8,72,768]{2,1,0:T(8,128)(2,1)S(1)}, u32[]{:S(2)}, u32[]{:S(2)}) %all-to-all-start.1) | async-done | bytes 884768 | tf_op jit(solution)/shard_map/all_to_all | solution.py:61
  107.4 7.8 %all-to-all-start.3 = ((bf16[16,64,384]{2,1,0:T(8,128)(2,1)}), bf16[16,64,384]{2,1,0:T(8,128)(2,1)S(1)}, u32[]{:S(2)}, u32[]{:S(2)}) async-start(bf16[16,64,384]{2,1,0:T(8,128)(2,1)} %broadcast_in_dim.23), calls=%async_computation.3 | async-start | bytes 1572864 | tf_op jit(solution)/shard_map/all_to_all | solution.py:33
  117.0 9.0 %collective-permute-done.9 = bf16[64,768]{1,0:T(8,128)(2,1)S(1)} collective-permute-done((bf16[64,768]{1,0:T(8,128)(2,1)S(1)}, bf16[64,768]{1,0:T(8,128)(2,1)S(1)}, u32[]{:S(2)}, u32[]{:S(2)}) %collective-permute-start.9) | collective-permute-done | bytes 98336 | tf_op jit(solution)/shard_map/ppermute | solution.py:131
  126.2 2.6 all-to-all-done.3
  128.8 1.9 stack.6
  130.7 19.5 %all-to-all-start.2 = ((bf16[16,64,1536]{2,1,0:T(8,128)(2,1)}), bf16[16,64,1536]{2,1,0:T(8,128)(2,1)S(1)}, u32[]{:S(2)}, u32[]{:S(2)}) async-start(bf16[16,64,1536]{2,1,0:T(8,128)(2,1)} %stack.6), calls=%async_computation.2 | async-start | bytes 6291456 | tf_op jit(solution)/shard_map/all_to_all | solution.py:133
  150.9 2.1 copy.12
  153.0 134.1 %all-to-all-done.2 = bf16[16,64,1536]{2,1,0:T(8,128)(2,1)S(1)} async-done(((bf16[16,64,1536]{2,1,0:T(8,128)(2,1)}), bf16[16,64,1536]{2,1,0:T(8,128)(2,1)S(1)}, u32[]{:S(2)}, u32[]{:S(2)}) %all-to-all-start.2) | async-done | bytes 3145760 | tf_op jit(solution)/shard_map/all_to_all | solution.py:133
  287.1 4.6 %multiply_reduce_fusion.2 = (f32[384]{0:T(512)S(1)}, f32[1536]{0:T(1024)S(1)}, f32[]{:T(128)}, f32[384,1536]{1,0:T(8,128)}) fusion(bf16[1024,384]{1,0:T(8,128)(2,1)} %bitcast.41, bf16[1024,1536]{1,0:T(8,128)(2,1)S(1)} %bitcast.33), kind=kOutput, calls=%fused_computation.3 | convolution fusion | flops 1210316928 | bytes 6299140 | tf_op jit(solution)/shard_map/dot_general | solution.py:27
  293.7 11.1 %all-to-all-start.4 = ((f32[16,16,128]{2,1,0:T(8,128)}), f32[16,16,128]{2,1,0:T(8,128)S(1)}, u32[]{:S(2)}, u32[]{:S(2)}) async-start(f32[16,16,128]{2,1,0:T(8,128)} %broadcast_in_dim.27), calls=%async_computation.4 | async-start | bytes 262144 | tf_op jit(solution)/shard_map/all_to_all | solution.py:33
  304.8 3.1 convolution_convert_fusion
  308.0 8.8 %all-to-all-done.4 = f32[16,16,128]{2,1,0:T(8,128)S(1)} async-done(((f32[16,16,128]{2,1,0:T(8,128)}), f32[16,16,128]{2,1,0:T(8,128)S(1)}, u32[]{:S(2)}, u32[]{:S(2)}) %all-to-all-start.4) | async-done | bytes 131104 | tf_op jit(solution)/shard_map/all_to_all | solution.py:33
  319.2 7.7 %all-to-all-start.5 = ((bf16[16,80,384]{2,1,0:T(8,128)(2,1)}), bf16[16,80,384]{2,1,0:T(8,128)(2,1)S(1)}, u32[]{:S(2)}, u32[]{:S(2)}) async-start(bf16[16,80,384]{2,1,0:T(8,128)(2,1)} %pad_maximum_fusion), calls=%async_computation.5 | async-start | bytes 1966080 | tf_op jit(solution)/shard_map/all_to_all | solution.py:33
  327.6 15.4 %all-to-all-done.5 = bf16[16,80,384]{2,1,0:T(8,128)(2,1)S(1)} async-done(((bf16[16,80,384]{2,1,0:T(8,128)(2,1)}), bf16[16,80,384]{2,1,0:T(8,128)(2,1)S(1)}, u32[]{:S(2)}, u32[]{:S(2)}) %all-to-all-start.5) | async-done | bytes 983072 | tf_op jit(solution)/shard_map/all_to_all | solution.py:33
  345.8 1.8 multiply_bitcast_fusion
  (87 shorter events, 28.0 us)
Async XLA Ops:
  0.6 17.6 %copy-start.4 = (bf16[32,384]{1,0:T(8,128)(2,1)S(1)}, bf16[32,384]{1,0:T(8,128)(2,1)}, u32[]{:S(2)}) copy-start(bf16[32,384]{1,0:T(8,128)(2,1)} %param.9) | copy-start | bytes 73732
  0.6 17.6 %copy-start.8 = (bf16[32,384]{1,0:T(8,128)(2,1)S(1)}, bf16[32,384]{1,0:T(8,128)(2,1)}, u32[]{:S(2)}) copy-start(bf16[32,384]{1,0:T(8,128)(2,1)} %param.8) | copy-start | bytes 73732
  0.7 17.6 %collective-permute-start = (bf16[32,384]{1,0:T(8,128)(2,1)}, bf16[32,384]{1,0:T(8,128)(2,1)S(1)}, u32[]{:S(2)}, u32[]{:S(2)}) collective-permute-start(bf16[32,384]{1,0:T(8,128)(2,1)} %param.9), channel_id=1, source_target_pairs={{0,256},{272,16},{32,288},{304,48},{64,320},{336,80},{96,352},{368... | collective-permute-start | bytes 73736 | tf_op jit(solution)/shard_map/ppermute | solution.py:94
  4.8 14.1 %collective-permute-start.1 = (bf16[32,384]{1,0:T(8,128)(2,1)}, bf16[32,384]{1,0:T(8,128)(2,1)S(1)}, u32[]{:S(2)}, u32[]{:S(2)}) collective-permute-start(bf16[32,384]{1,0:T(8,128)(2,1)} %param.9), channel_id=1, source_target_pairs={{16,0},{256,272},{48,32},{288,304},{80,64},{320,336},{112,96},{352... | collective-permute-start | bytes 73736 | tf_op jit(solution)/shard_map/ppermute | solution.py:95
  6.1 12.8 %collective-permute-start.2 = (bf16[32,384]{1,0:T(8,128)(2,1)}, bf16[32,384]{1,0:T(8,128)(2,1)S(1)}, u32[]{:S(2)}, u32[]{:S(2)}) collective-permute-start(bf16[32,384]{1,0:T(8,128)(2,1)} %param.9), channel_id=1, source_target_pairs={{16,256},{256,16},{48,288},{288,48},{80,320},{320,80},{112,352},{3... | collective-permute-start | bytes 73736 | tf_op jit(solution)/shard_map/ppermute | solution.py:96
  7.5 9.2 %collective-permute-start.11 = (bf16[32,384]{1,0:T(8,128)(2,1)S(1)}, bf16[32,384]{1,0:T(8,128)(2,1)S(1)}, u32[]{:S(2)}, u32[]{:S(2)}) collective-permute-start(bf16[32,384]{1,0:T(8,128)(2,1)S(1)} %broadcast_select_fusion.10), channel_id=1, source_target_pairs={{0,256},{256,0},{1,257},{257,1},{2,258},{258,2},{3,259},{259,3},{4... | collective-permute-start | bytes 73736 | tf_op jit(solution)/shard_map/ppermute | solution.py:140
  15.3 35.0 %collective-permute-start.7 = (bf16[384,768]{1,0:T(8,128)(2,1)S(1)}, bf16[384,768]{1,0:T(8,128)(2,1)}, u32[]{:S(2)}, u32[]{:S(2)}) collective-permute-start(bf16[384,768]{1,0:T(8,128)(2,1)S(1)} %get-tuple-element.16), channel_id=1, source_target_pairs={{256,16},{272,0},{288,48},{304,32},{320,80},{336,64},{352,112},{36... | collective-permute-start | bytes 1769480 | tf_op jit(solution)/shard_map/ppermute | solution.py:104
  16.8 33.5 %collective-permute-start.8 = (bf16[384,768]{1,0:T(8,128)(2,1)S(1)}, bf16[384,768]{1,0:T(8,128)(2,1)}, u32[]{:S(2)}, u32[]{:S(2)}) collective-permute-start(bf16[384,768]{1,0:T(8,128)(2,1)S(1)} %get-tuple-element.15), channel_id=1, source_target_pairs={{256,272},{272,256},{288,304},{304,288},{320,336},{336,320},{352,3... | collective-permute-start | bytes 1769480 | tf_op jit(solution)/shard_map/ppermute | solution.py:100
  19.9 30.4 %all-to-all-start = ((bf16[16,32,768]{2,1,0:T(8,128)(2,1)}), bf16[16,32,768]{2,1,0:T(8,128)(2,1)S(1)}, u32[]{:S(2)}, u32[]{:S(2)}) async-start(bf16[16,32,768]{2,1,0:T(8,128)(2,1)} %broadcast_in_dim.22), calls=%async_computation | async-start | bytes 1572864 | tf_op jit(solution)/shard_map/all_to_all | solution.py:33
  28.3 29.5 %copy-start.1 = (bf16[1,384,1536]{2,1,0:T(8,128)(2,1)S(1)}, bf16[1,384,1536]{2,1,0:T(8,128)(2,1)}, u32[]{:S(2)}) copy-start(bf16[1,384,1536]{2,1,0:T(8,128)(2,1)} %param.6) | copy-start | bytes 3538948
  28.4 12.6 %collective-permute-start.3 = (bf16[32,768]{1,0:T(8,128)(2,1)S(1)}, bf16[32,768]{1,0:T(8,128)(2,1)S(1)}, u32[]{:S(2)}, u32[]{:S(2)}) collective-permute-start(bf16[32,768]{1,0:T(8,128)(2,1)S(1)} %broadcast_select_fusion.2), channel_id=1, source_target_pairs={{0,256},{272,16},{32,288},{304,48},{64,320},{336,80},{96,352},{368... | collective-permute-start | bytes 147464 | tf_op jit(solution)/shard_map/ppermute | solution.py:94
  35.4 7.6 %collective-permute-start.5 = (bf16[32,768]{1,0:T(8,128)(2,1)S(1)}, bf16[32,768]{1,0:T(8,128)(2,1)S(1)}, u32[]{:S(2)}, u32[]{:S(2)}) collective-permute-start(bf16[32,768]{1,0:T(8,128)(2,1)S(1)} %broadcast_select_fusion.2), channel_id=1, source_target_pairs={{16,256},{256,16},{48,288},{288,48},{80,320},{320,80},{112,352},{3... | collective-permute-start | bytes 147464 | tf_op jit(solution)/shard_map/ppermute | solution.py:96
  36.1 21.8 %collective-permute-start.6 = (bf16[384,768]{1,0:T(8,128)(2,1)S(1)}, bf16[384,768]{1,0:T(8,128)(2,1)}, u32[]{:S(2)}, u32[]{:S(2)}) collective-permute-start(bf16[384,768]{1,0:T(8,128)(2,1)S(1)} %get-tuple-element.16), channel_id=1, source_target_pairs={{256,0},{272,16},{288,32},{304,48},{320,64},{336,80},{352,96},{368... | collective-permute-start | bytes 1769480 | tf_op jit(solution)/shard_map/ppermute | solution.py:103
  41.7 8.0 %collective-permute-start.4 = (bf16[32,768]{1,0:T(8,128)(2,1)S(1)}, bf16[32,768]{1,0:T(8,128)(2,1)S(1)}, u32[]{:S(2)}, u32[]{:S(2)}) collective-permute-start(bf16[32,768]{1,0:T(8,128)(2,1)S(1)} %get-tuple-element.14), channel_id=1, source_target_pairs={{16,0},{256,272},{48,32},{288,304},{80,64},{320,336},{112,96},{352... | collective-permute-start | bytes 147464 | tf_op jit(solution)/shard_map/ppermute | solution.py:95
  62.1 44.3 %all-to-all-start.1 = ((f16[8,72,768]{2,1,0:T(8,128)(2,1)}), f16[8,72,768]{2,1,0:T(8,128)(2,1)S(1)}, u32[]{:S(2)}, u32[]{:S(2)}) async-start(f16[8,72,768]{2,1,0:T(8,128)(2,1)} %concatenate.29), calls=%async_computation.1 | async-start | bytes 1769472 | tf_op jit(solution)/shard_map/all_to_all | solution.py:61
  75.8 41.2 %collective-permute-start.10 = (bf16[64,768]{1,0:T(8,128)(2,1)S(1)}, bf16[64,768]{1,0:T(8,128)(2,1)S(1)}, u32[]{:S(2)}, u32[]{:S(2)}) collective-permute-start(bf16[64,768]{1,0:T(8,128)(2,1)S(1)} %pad_maximum_fusion.1), channel_id=1, source_target_pairs={{0,256},{1,257},{2,258},{3,259},{4,260},{5,261},{6,262},{7,263},{8... | collective-permute-start | bytes 294920 | tf_op jit(solution)/shard_map/ppermute | solution.py:126
  107.4 21.4 %all-to-all-start.3 = ((bf16[16,64,384]{2,1,0:T(8,128)(2,1)}), bf16[16,64,384]{2,1,0:T(8,128)(2,1)S(1)}, u32[]{:S(2)}, u32[]{:S(2)}) async-start(bf16[16,64,384]{2,1,0:T(8,128)(2,1)} %broadcast_in_dim.23), calls=%async_computation.3 | async-start | bytes 1572864 | tf_op jit(solution)/shard_map/all_to_all | solution.py:33
  115.7 10.3 %collective-permute-start.9 = (bf16[64,768]{1,0:T(8,128)(2,1)S(1)}, bf16[64,768]{1,0:T(8,128)(2,1)S(1)}, u32[]{:S(2)}, u32[]{:S(2)}) collective-permute-start(bf16[64,768]{1,0:T(8,128)(2,1)S(1)} %fusion.19), channel_id=1, source_target_pairs={{256,0},{257,1},{258,2},{259,3},{260,4},{261,5},{262,6},{263,7},{2... | collective-permute-start | bytes 294920 | tf_op jit(solution)/shard_map/ppermute | solution.py:131
  130.7 19.6 %copy-start.12 = (f32[1,384]{1,0:T(1,128)S(1)}, f32[1,384]{1,0:T(1,128)}, u32[]{:S(2)}) copy-start(f32[1,384]{1,0:T(1,128)} %param.10) | copy-start | bytes 4612
  130.7 156.4 %all-to-all-start.2 = ((bf16[16,64,1536]{2,1,0:T(8,128)(2,1)}), bf16[16,64,1536]{2,1,0:T(8,128)(2,1)S(1)}, u32[]{:S(2)}, u32[]{:S(2)}) async-start(bf16[16,64,1536]{2,1,0:T(8,128)(2,1)} %stack.6), calls=%async_computation.2 | async-start | bytes 6291456 | tf_op jit(solution)/shard_map/all_to_all | solution.py:133
  293.7 23.1 %all-to-all-start.4 = ((f32[16,16,128]{2,1,0:T(8,128)}), f32[16,16,128]{2,1,0:T(8,128)S(1)}, u32[]{:S(2)}, u32[]{:S(2)}) async-start(f32[16,16,128]{2,1,0:T(8,128)} %broadcast_in_dim.27), calls=%async_computation.4 | async-start | bytes 262144 | tf_op jit(solution)/shard_map/all_to_all | solution.py:33
  319.2 26.6 %copy-start.2 = (f32[384,1536]{1,0:T(8,128)S(1)}, f32[384,1536]{1,0:T(8,128)}, u32[]{:S(2)}) copy-start(f32[384,1536]{1,0:T(8,128)} %get-tuple-element.26) | copy-start | bytes 7077892
  319.2 23.9 %all-to-all-start.5 = ((bf16[16,80,384]{2,1,0:T(8,128)(2,1)}), bf16[16,80,384]{2,1,0:T(8,128)(2,1)S(1)}, u32[]{:S(2)}, u32[]{:S(2)}) async-start(bf16[16,80,384]{2,1,0:T(8,128)(2,1)} %pad_maximum_fusion), calls=%async_computation.5 | async-start | bytes 1966080 | tf_op jit(solution)/shard_map/all_to_all | solution.py:33
  343.9 3.8 %collective-permute-start.12 = (f32[32,384]{1,0:T(8,128)S(1)}, f32[32,384]{1,0:T(8,128)S(1)}, u32[]{:S(2)}, u32[]{:S(2)}) collective-permute-start(f32[32,384]{1,0:T(8,128)S(1)} %slice.71), channel_id=1, source_target_pairs={{0,256},{1,257},{2,258},{3,259},{4,260},{5,261},{6,262},{7,263},{8... | collective-permute-start | bytes 147464 | tf_op jit(solution)/shard_map/ppermute | solution.py:171
  (8 other events, 84.9 us)
